TPU v7x, 32 devices: a whole 2x2x4 slice. The times are simulated.
32 devices in a mesh: tile: 16 (over z, y, x), mode: 2 (over core).
Axes of the slice: x: 2, y: 2, z: 4, core: 2. Of those that a mesh axis runs over, the one named last changes fastest.
Arguments:
- object_tiles: float32 [2, 2048, 2048], P(None, 'tile'), may hold values from -6 to 6
- probe_modes: float32 [4, 2, 256, 256], P('mode'), may hold values from -5 to 5
- amplitudes: float32 [16, 256, 256], P('tile'), may hold values from 0.25 to 4
- scan_offsets: int32 [8192, 2], replicated, may hold values from 0 to 1792, as said below
- slot_scan: int32 [16], P('tile'), may hold values from 0 to 8191, as said below
- slot_count: int32 [16], P('tile'), may hold values from 0 to 1, as said below
Outputs:
- updated_object: float32 [2, 2048, 2048], P(None, 'tile')
- object_gradient: float32 [2, 2048, 2048], P(None, 'tile')
Inputs may be any that keep to these rules, and one draw needn't show every extreme that they name: `scan_offsets`: every patch of 256 x 256 pixels at an offset lies inside the object. `slot_scan`: on every index d of tile but the last, the row offset of each slot's scan position lies in [d * 128, (d + 1) * 128). The positions of one device's slots are distinct. `slot_count`: the live slots of a device are its first ones. The last index of tile holds none, every other holds at least one; some index holds 1.
All inputs are finite; a program needn't handle non-finite values.
Results may differ from a plain program's by a relative error of at most 0.0001.
Values sent between devices are 32-bit elements; how exact they have to be, the bound alone decides.
No kernel may reach another device: no remote copies, remote signals or barrier semaphores. Data moves between devices by JAX's collectives and lax.ppermute only.
A program may use at most 64 MiB of HBM per device.

v0:
```python
import math
import jax
import jax.numpy as jnp
from jax import lax
from jax.sharding import PartitionSpec as P

FLOOR = 0.25
ALPHA = 0.5


def from_behind(value, axis, steps):
    count = lax.axis_size(axis)
    initial, last = (max(0, -steps), min(count, count - steps))
    return lax.ppermute(value, axis, [(source, source + steps) for source in range(initial, last)])


def tables(frame):
    index = jnp.arange(frame, dtype=jnp.int32)
    phase = (index[:, None] * index[None, :] % frame).astype(jnp.float32) * (2.0 * math.pi / frame)
    scale = 1.0 / math.sqrt(frame)
    return (jnp.cos(phase) * scale, -jnp.sin(phase) * scale)


def product(first, second):
    return jnp.matmul(first, second, precision=lax.Precision.HIGHEST)


def transform(real_part, imag_part, cos_table, sin_table):
    inner_re = product(cos_table, real_part) - product(sin_table, imag_part)
    inner_im = product(cos_table, imag_part) + product(sin_table, real_part)
    outer_re = product(inner_re, cos_table) - product(inner_im, sin_table)
    outer_im = product(inner_im, cos_table) + product(inner_re, sin_table)
    return (outer_re, outer_im)


def shards(object_tiles, probe_modes, amplitudes, scan_offsets, slot_scan, slot_count):
    height = object_tiles.shape[1]
    breadth = object_tiles.shape[2]
    frame = probe_modes.shape[2]
    slot_total = slot_scan.shape[0]
    device = lax.axis_index("tile")
    anchor = jnp.zeros((), jnp.int32)
    cos_table, sin_table = tables(frame)
    probe_re = probe_modes[:, 0]
    probe_im = probe_modes[:, 1]
    illumination = lax.psum(jnp.sum(probe_re * probe_re + probe_im * probe_im, axis=0), "mode")
    offsets = jnp.take(scan_offsets, slot_scan, axis=0)
    row_start = offsets[:, 0] - device * height
    col_start = offsets[:, 1]
    active = (jnp.arange(slot_total, dtype=jnp.int32) < slot_count[0]).astype(jnp.float32)

    def cut_columns(col_at):
        return lax.dynamic_slice(object_tiles, (anchor, anchor, col_at), (2, height, frame))

    their_starts = []
    pieces = [jax.vmap(cut_columns)(col_start)]
    for distance in (1, 2):
        remote = from_behind(col_start, "tile", distance)
        their_starts.append(remote)
        windows = jax.vmap(cut_columns)(remote)
        pieces.append(from_behind(windows, "tile", -distance))
    canvas = jnp.concatenate(pieces, axis=2)

    def cut_rows(column_block, row_at):
        return lax.dynamic_slice(column_block, (anchor, row_at, anchor), (2, frame, frame))

    patches = jax.vmap(cut_rows)(canvas, row_start)
    patch_re = patches[:, 0][:, None]
    patch_im = patches[:, 1][:, None]
    wave_re = probe_re[None] * patch_re - probe_im[None] * patch_im
    wave_im = probe_re[None] * patch_im + probe_im[None] * patch_re
    far_re, far_im = transform(wave_re, wave_im, cos_table, sin_table)
    intensity = lax.psum(jnp.sum(far_re * far_re + far_im * far_im, axis=1), "mode")
    factor = (amplitudes / jnp.sqrt(jnp.maximum(intensity, FLOOR)))[:, None]
    back_re, back_im = transform(far_re * factor, far_im * factor, cos_table, -sin_table)
    delta_re = back_re - wave_re
    delta_im = back_im - wave_im
    weights = active[:, None, None]
    grad_re = jnp.sum(probe_re[None] * delta_re + probe_im[None] * delta_im, axis=1) * weights
    grad_im = jnp.sum(probe_re[None] * delta_im - probe_im[None] * delta_re, axis=1) * weights
    coverage = illumination[None] * weights
    contribution = jnp.stack([grad_re, grad_im, coverage], axis=1)
    channels = contribution.shape[1]

    def place(piece, row_at):
        empty = jnp.zeros((channels, 3 * height, frame), jnp.float32)
        return lax.dynamic_update_slice(empty, piece, (anchor, row_at, anchor))

    padded = jax.vmap(place)(contribution, row_start)
    blocks = [(padded[:, :, :height], col_start)]
    for distance in (1, 2):
        arrived = from_behind(
            padded[:, :, distance * height : (distance + 1) * height], "tile", distance
        )
        blocks.append((arrived, their_starts[distance - 1]))
    totals = jnp.zeros((channels, height, breadth), jnp.float32)
    for block, starts in blocks:

        def add_block(index, accum, block=block, starts=starts):
            current = lax.dynamic_slice(
                accum, (anchor, anchor, starts[index]), (channels, height, frame)
            )
            return lax.dynamic_update_slice(
                accum, current + block[index], (anchor, anchor, starts[index])
            )

        totals = lax.fori_loop(0, slot_total, add_block, totals)
    cover = totals[2]
    gradient = totals[:2]
    gradient = lax.psum(gradient, "mode")
    updated = object_tiles + gradient / (cover + ALPHA)
    return (updated, gradient)


def solution(mesh):
    return jax.shard_map(
        shards,
        mesh=mesh,
        in_specs=(
            P(None, "tile", None),
            P("mode", None, None, None),
            P("tile", None, None),
            P(),
            P("tile"),
            P("tile"),
        ),
        out_specs=(P(None, "tile", None), P(None, "tile", None)),
        check_vma=False,
    )
```

profile of v0, /device:TPU:0, one launch (start us, length us, event | category | flops | bytes accessed | tf_op | source)
XLA Modules:
  0.0 183.3 jit_solution(3276640202237334104)
XLA Ops:
  9.2 5.5 %collective-permute-start.2 = (s32[1]{0:T(128)}, s32[1]{0:T(128)}, u32[]{:S(2)}, u32[]{:S(2)}) collective-permute-start(s32[1]{0:T(128)} %bitcast.10), channel_id=1, source_target_pairs={{0,4},{2,6},{4,8},{6,10},{8,12},{10,14},{12,16},{14,18},{16,20},{1... | collective-permute-start | bytes 20 | tf_op jit(solution)/shard_map/ppermute | solution.py:14
  14.7 3.9 %collective-permute-start = (s32[1]{0:T(128)}, s32[1]{0:T(128)}, u32[]{:S(2)}, u32[]{:S(2)}) collective-permute-start(s32[1]{0:T(128)} %bitcast.10), channel_id=1, source_target_pairs={{0,2},{2,4},{4,6},{6,8},{8,10},{10,12},{12,14},{14,16},{16,18},{18... | collective-permute-start | bytes 20 | tf_op jit(solution)/shard_map/ppermute | solution.py:14
  24.1 1.7 dynamic-slice_bitcast_fusion
  29.1 6.1 %collective-permute-done.3 = f32[1,2,128,256]{3,2,1,0:T(8,128)S(1)} collective-permute-done((f32[1,2,128,256]{3,2,1,0:T(8,128)S(1)}, f32[1,2,128,256]{3,2,1,0:T(8,128)S(1)}, u32[]{:S(2)}, u32[]{:S(2)}) %collective-permute-start.3) | collective-permute-done | bytes 262176 | tf_op jit(solution)/shard_map/ppermute | solution.py:14
  36.9 1.6 fusion.46
  38.6 1.6 fusion.42
  43.4 1.6 fusion.4
  48.2 2.5 %add_reduce_fusion = (f32[256,256]{1,0:T(8,128)}, f32[2,256,256]{2,1,0:T(8,128)S(1)}) fusion(f32[2,256,256]{2,1,0:T(8,128)S(1)} %convolution_subtract_fusion.2, f32[2,256,256]{2,1,0:T(8,128)S(1)} %fusion.40, f32[2,256,256]{2,1,0:T(8,128)S(1)} %fusion.5), kind=kOutput, calls=%fused_computation.41 | convolution fusion | flops 404291584 | bytes 2359296 | tf_op jit(solution)/shard_map/dot_general | solution.py:25
  51.5 21.8 %all-reduce.7.cloned.1.call-done = f32[1,256,256]{2,1,0:T(8,128)} async-done(((f32[1,256,256]{2,1,0:T(8,128)}), f32[1,256,256]{2,1,0:T(8,128)}) %all-reduce.7.cloned.1.call-update) | async-done | bytes 262160 | tf_op jit(solution)/shard_map/psum | solution.py:73
  74.3 1.6 fusion.21
  76.0 1.7 fusion.17
  77.6 1.7 fusion.2
  79.3 1.7 fusion.3
  85.7 2.6 %fusion.12 = (f32[256,256]{1,0:T(8,128)S(1)}, f32[256,256]{1,0:T(8,128)S(1)}, f32[256,256]{1,0:T(8,128)}) fusion(f32[2,256,256]{2,1,0:T(8,128)S(1)} %fusion.1, f32[2,2,256,256]{3,2,1,0:T(8,128)S(1)} %copy-done.1, f32[2,256,256]{2,1,0:T(8,128)S(1)} %get-tuple-element.121, f32[2,256,256]{2,1,0:T(8,128)S(1)} %fusion.34, f32[2,256,256]{2,1,0:T(8,128)S(1)} %fusion.3), kind=kOutput, calls=%fused_computation.31 | convolution fusion | flops 405405696 | bytes 3932160 | tf_op jit(solution)/shard_map/dot_general | solution.py:25
  88.4 2.7 %and_reduce_fusion = pred[]{:T(512)} fusion(s32[4]{0:T(128)S(1)} %copy-done.3, s32[1]{0:T(128)} %bitcast.7, s32[1]{0:T(128)} %bitcast.6, s32[1]{0:T(128)} %bitcast.5, s32[1]{0:T(128)} %constant.96.clone.1), kind=kLoop, calls=%fused_computation.118 | loop fusion | flops 27 | bytes 33 | tf_op jit(solution)/shard_map/reduce.1
  91.8 16.2 %all-reduce.9.cloned.1.call-done = f32[256,256]{1,0:T(8,128)} async-done(((f32[256,256]{1,0:T(8,128)}), f32[256,256]{1,0:T(8,128)}) %all-reduce.9.cloned.1.call-update) | async-done | bytes 262160 | tf_op jit(solution)/shard_map/psum | solution.py:46
  109.7 4.8 %scatter.4 = f32[1,3,384,256]{3,2,1,0:T(8,128)S(1)} dynamic-update-slice(f32[1,3,384,256]{3,2,1,0:T(8,128)S(1)} %broadcast_in_dim.32, f32[1,3,256,256]{3,2,1,0:T(8,128)S(1)} %maximum_select_fusion, s32[]{:T(128)} %constant.95.clone.1, s32[]{:T(128)} %constant.95.clone.1, s32[]{:T(128)} %bitcast.49, s32[]{:T(128)} %constant.95.clone.1) | dynamic-update-slice | bytes 1572868 | tf_op jit(solution)/shard_map/vmap(vmap())/scatter | solution.py:87
  115.5 3.8 %collective-permute-start.4 = (f32[1,3,128,256]{3,2,1,0:T(8,128)}, f32[1,3,128,256]{3,2,1,0:T(8,128)}, u32[]{:S(2)}, u32[]{:S(2)}) collective-permute-start(f32[1,3,128,256]{3,2,1,0:T(8,128)} %get-tuple-element.123), channel_id=1, source_target_pairs={{0,2},{2,4},{4,6},{6,8},{8,10},{10,12},{12,14},{14,16},{16,18},{18... | collective-permute-start | bytes 1179656 | tf_op jit(solution)/shard_map/ppermute | solution.py:14
  119.3 3.8 %collective-permute-start.5 = (f32[1,3,128,256]{3,2,1,0:T(8,128)}, f32[1,3,128,256]{3,2,1,0:T(8,128)}, u32[]{:S(2)}, u32[]{:S(2)}) collective-permute-start(f32[1,3,128,256]{3,2,1,0:T(8,128)} %get-tuple-element.122), channel_id=1, source_target_pairs={{0,4},{2,6},{4,8},{6,10},{8,12},{10,14},{12,16},{14,18},{16,20},{1... | collective-permute-start | bytes 1179656 | tf_op jit(solution)/shard_map/ppermute | solution.py:14
  128.9 4.8 %dynamic_update_slice.12 = f32[3,128,2048]{2,1,0:T(8,128)S(1)} dynamic-update-slice(f32[3,128,2048]{2,1,0:T(8,128)S(1)} %broadcast_in_dim.31, f32[3,128,256]{2,1,0:T(8,128)S(1)} %get-tuple-element.124, s32[]{:T(128)} %constant.95.clone.1, s32[]{:T(128)} %constant.95.clone.1, s32[]{:T(128)S(6)} %select_n.101) | dynamic-update-slice | bytes 786436 | tf_op jit(solution)/shard_map/while/body/eval_jaxpr/dynamic_update_slice | solution.py:103
  134.9 4.8 %dynamic_update_slice.13 = f32[3,128,2048]{2,1,0:T(8,128)S(1)} dynamic-update-slice(f32[3,128,2048]{2,1,0:T(8,128)S(1)} %dynamic_update_slice.12, f32[3,128,256]{2,1,0:T(8,128)S(1)} %bitcast_add_fusion.1, s32[]{:T(128)} %constant.95.clone.1, s32[]{:T(128)} %constant.95.clone.1, s32[]{:T(128)S(6)} %select_n.102) | dynamic-update-slice | bytes 786436 | tf_op jit(solution)/shard_map/while/body/eval_jaxpr/dynamic_update_slice | solution.py:103
  141.0 4.8 %dynamic_update_slice.14 = f32[3,128,2048]{2,1,0:T(8,128)S(1)} dynamic-update-slice(f32[3,128,2048]{2,1,0:T(8,128)S(1)} %dynamic_update_slice.13, f32[3,128,256]{2,1,0:T(8,128)S(1)} %bitcast_add_fusion, s32[]{:T(128)} %constant.95.clone.1, s32[]{:T(128)} %constant.95.clone.1, s32[]{:T(128)S(6)} %select_n.103) | dynamic-update-slice | bytes 786436 | tf_op jit(solution)/shard_map/while/body/eval_jaxpr/dynamic_update_slice | solution.py:103
  148.3 22.6 %all-reduce.11.cloned.1.call-done = f32[2,128,2048]{2,1,0:T(8,128)} async-done(((f32[2,128,2048]{2,1,0:T(8,128)}), f32[2,128,2048]{2,1,0:T(8,128)}) %all-reduce.11.cloned.1.call-update) | async-done | bytes 2097168 | tf_op jit(solution)/shard_map/psum | solution.py:110
  171.0 4.5 %divide_add_fusion = f32[2,128,2048]{2,1,0:T(8,128)} fusion(f32[2,128,2048]{2,1,0:T(8,128)} %param.8, f32[2,128,2048]{2,1,0:T(8,128)} %all-reduce.11.cloned.1.call-done, f32[128,2048]{1,0:T(8,128)} %fusion.6), kind=kLoop, calls=%fused_computation | loop fusion | flops 1048576 | bytes 7340032 | tf_op jit(solution)/shard_map/add | solution.py:111
  (49 shorter events, 27.8 us)
Async XLA Ops:
  7.2 29.6 %copy-start.1 = (f32[2,2,256,256]{3,2,1,0:T(8,128)S(1)}, f32[2,2,256,256]{3,2,1,0:T(8,128)}, u32[]{:S(2)}) copy-start(f32[2,2,256,256]{3,2,1,0:T(8,128)} %param.9) | copy-start | bytes 3145732
  7.2 66.1 %all-reduce.7.cloned.1.call-start = ((), (), s32[]{:S(2)}) async-start(), calls=%async_computation | async-start | bytes 524288 | tf_op jit(solution)/shard_map/psum | solution.py:73
  9.2 11.1 %collective-permute-start.2 = (s32[1]{0:T(128)}, s32[1]{0:T(128)}, u32[]{:S(2)}, u32[]{:S(2)}) collective-permute-start(s32[1]{0:T(128)} %bitcast.10), channel_id=1, source_target_pairs={{0,4},{2,6},{4,8},{6,10},{8,12},{10,14},{12,16},{14,18},{16,20},{1... | collective-permute-start | bytes 20 | tf_op jit(solution)/shard_map/ppermute | solution.py:14
  14.7 7.0 %collective-permute-start = (s32[1]{0:T(128)}, s32[1]{0:T(128)}, u32[]{:S(2)}, u32[]{:S(2)}) collective-permute-start(s32[1]{0:T(128)} %bitcast.10), channel_id=1, source_target_pairs={{0,2},{2,4},{4,6},{6,8},{8,10},{10,12},{12,14},{14,16},{16,18},{18... | collective-permute-start | bytes 20 | tf_op jit(solution)/shard_map/ppermute | solution.py:14
  25.8 9.4 %collective-permute-start.3 = (f32[1,2,128,256]{3,2,1,0:T(8,128)S(1)}, f32[1,2,128,256]{3,2,1,0:T(8,128)S(1)}, u32[]{:S(2)}, u32[]{:S(2)}) collective-permute-start(f32[1,2,128,256]{3,2,1,0:T(8,128)S(1)} %get-tuple-element.117), channel_id=1, source_target_pairs={{4,0},{6,2},{8,4},{10,6},{12,8},{14,10},{16,12},{18,14},{20,16},{2... | collective-permute-start | bytes 786440 | tf_op jit(solution)/shard_map/ppermute | solution.py:14
  27.1 9.4 %collective-permute-start.1 = (f32[1,2,128,256]{3,2,1,0:T(8,128)S(1)}, f32[1,2,128,256]{3,2,1,0:T(8,128)S(1)}, u32[]{:S(2)}, u32[]{:S(2)}) collective-permute-start(f32[1,2,128,256]{3,2,1,0:T(8,128)S(1)} %get-tuple-element.118), channel_id=1, source_target_pairs={{2,0},{4,2},{6,4},{8,6},{10,8},{12,10},{14,12},{16,14},{18,16},{20... | collective-permute-start | bytes 786440 | tf_op jit(solution)/shard_map/ppermute | solution.py:14
  46.6 4.1 %copy-start.4 = (s32[1,3]{1,0:T(1,128)S(1)}, s32[1,3]{1,0:T(1,128)}, u32[]{:S(2)}) copy-start(s32[1,3]{1,0:T(1,128)} %constant.105.clone.1) | copy-start | bytes 40
  46.7 26.7 %copy-start.2 = (f32[1,256,256]{2,1,0:T(8,128)S(1)}, f32[1,256,256]{2,1,0:T(8,128)}, u32[]{:S(2)}) copy-start(f32[1,256,256]{2,1,0:T(8,128)} %param.10) | copy-start | bytes 786436
  50.7 57.2 %all-reduce.9.cloned.1.call-start = ((), (), s32[]{:S(2)}) async-start(), calls=%async_computation.1 | async-start | bytes 524288 | tf_op jit(solution)/shard_map/psum | solution.py:46
  85.7 2.7 %copy-start.3 = (s32[4]{0:T(128)S(1)}, s32[4]{0:T(128)}, u32[]{:S(2)}) copy-start(s32[4]{0:T(128)} %constant.106.clone.1) | copy-start | bytes 52
  88.3 82.6 %all-reduce.11.cloned.1.call-start = ((), (), s32[]{:S(2)}) async-start(), calls=%async_computation.2 | async-start | bytes 4194304 | tf_op jit(solution)/shard_map/psum | solution.py:110
  115.5 18.3 %collective-permute-start.4 = (f32[1,3,128,256]{3,2,1,0:T(8,128)}, f32[1,3,128,256]{3,2,1,0:T(8,128)}, u32[]{:S(2)}, u32[]{:S(2)}) collective-permute-start(f32[1,3,128,256]{3,2,1,0:T(8,128)} %get-tuple-element.123), channel_id=1, source_target_pairs={{0,2},{2,4},{4,6},{6,8},{8,10},{10,12},{12,14},{14,16},{16,18},{18... | collective-permute-start | bytes 1179656 | tf_op jit(solution)/shard_map/ppermute | solution.py:14
  119.3 20.5 %collective-permute-start.5 = (f32[1,3,128,256]{3,2,1,0:T(8,128)}, f32[1,3,128,256]{3,2,1,0:T(8,128)}, u32[]{:S(2)}, u32[]{:S(2)}) collective-permute-start(f32[1,3,128,256]{3,2,1,0:T(8,128)} %get-tuple-element.122), channel_id=1, source_target_pairs={{0,4},{2,6},{4,8},{6,10},{8,12},{10,14},{12,16},{14,18},{16,20},{1... | collective-permute-start | bytes 1179656 | tf_op jit(solution)/shard_map/ppermute | solution.py:14
  170.9 4.5 %copy-start = (f32[2,128,2048]{2,1,0:T(8,128)S(1)}, f32[2,128,2048]{2,1,0:T(8,128)}, u32[]{:S(2)}) copy-start(f32[2,128,2048]{2,1,0:T(8,128)} %all-reduce.11.cloned.1.call-done) | copy-start | bytes 6291460
Sparse Core Ops, SparseCore 0:
  50.9 22.4 all-reduce.6
  88.5 19.4 all-reduce.8
  147.4 23.5 all-reduce.10
where the time goes:
time: 184 us; the launch traced here: 183 us
  waiting for transfers between devices  68.1 us (37%)
  matrix products  27.6 us (15%)
  between operations  27.1 us (15%)
  local copies, waits for them, and re-layouts  26.4 us (14%)
  starting transfers between devices  19.7 us (11%)
  other arithmetic  14.4 us (8%)
    dot_general x16, matrix products, product(): return jnp.matmul(first, second, precision=lax.Precision.HIGHEST)  27.6 us
    psum x1, waiting for transfers between devices, shards(): gradient = lax.psum(gradient, 'mode')  22.6 us
    psum x1, waiting for transfers between devices, shards(): lax.psum(jnp.sum(far_re * far_re + far_im * far_im, axis=1), 'mode')  21.8 us
    ppermute x6, starting transfers between devices, from_behind(): lax.ppermute(value, axis, [(source, source + steps) for source in range(i...  19.6 us
    psum x1, waiting for transfers between devices, shards(): lax.psum(jnp.sum(probe_re * probe_re + probe_im * probe_im, axis=0), 'mode')  16.2 us
    dynamic_update_slice x3, local copies, waits for them, and re-layouts, add_block(): lax.dynamic_update_slice(accum, current + block[index], (anchor, anchor,...  14.5 us
    ppermute x6, waiting for transfers between devices, from_behind(): lax.ppermute(value, axis, [(source, source + steps) for source in range(i...  7.43 us
    scatter x1, local copies, waits for them, and re-layouts, place(): return lax.dynamic_update_slice(empty, piece, (anchor, row_at, anchor))  4.77 us
  transfers between devices with their start and end apart: 9, of which 5 were waited for; matrix products, arithmetic and copies ran while one was open for 9% of the time, Pallas kernels for 0%

commit v1 on v0

--- a/solution.py
+++ b/solution.py
@@ -43,7 +43,9 @@
     cos_table, sin_table = tables(frame)
     probe_re = probe_modes[:, 0]
     probe_im = probe_modes[:, 1]
-    illumination = lax.psum(jnp.sum(probe_re * probe_re + probe_im * probe_im, axis=0), "mode")
+    illumination = jnp.sum(
+        lax.all_gather(jnp.sum(probe_re * probe_re + probe_im * probe_im, axis=0), "mode"), axis=0
+    )
     offsets = jnp.take(scan_offsets, slot_scan, axis=0)
     row_start = offsets[:, 0] - device * height
     col_start = offsets[:, 1]

time: 184 us -> 166 us (0.902)
  waiting for transfers between devices: 68.1 us -> 48.5 us
  blocking collectives: 0 us -> 2.18 us
    psum x1 -> x0, waiting for transfers between devices: 16.2 us -> none  [shards(): lax.psum(jnp.sum(probe_re * probe_re + probe_im * probe_im, axis=0), 'mode')]
    psum x1, waiting for transfers between devices: 21.8 us -> 18.5 us  [shards(): lax.psum(jnp.sum(far_re * far_re + far_im * far_im, axis=1), 'mode')]
    all_gather x0 -> x1, blocking collectives: none -> 2.18 us  [shards(): lax.all_gather(jnp.sum(probe_re * probe_re + probe_im * probe_im, axis=0)...]
  transfers between devices with their start and end apart: 9 -> 8, of which waited for: 5 -> 4; matrix products, arithmetic and copies ran while one was open for 9% -> 9% of each run, Pallas kernels for 0% -> 0%
where the time goes in v1:
time: 166 us; the launch traced here: 165 us
  waiting for transfers between devices  48.5 us (29%)
  between operations  27.7 us (17%)
  matrix products  26.9 us (16%)
  local copies, waits for them, and re-layouts  26.5 us (16%)
  starting transfers between devices  19.6 us (12%)
  other arithmetic  13.5 us (8%)
  blocking collectives  2.18 us (1%)
    dot_general x16, matrix products, product(): return jnp.matmul(first, second, precision=lax.Precision.HIGHEST)  26.9 us
    psum x1, waiting for transfers between devices, shards(): gradient = lax.psum(gradient, 'mode')  22.5 us
    ppermute x6, starting transfers between devices, from_behind(): lax.ppermute(value, axis, [(source, source + steps) for source in range(i...  19.5 us
    psum x1, waiting for transfers between devices, shards(): lax.psum(jnp.sum(far_re * far_re + far_im * far_im, axis=1), 'mode')  18.5 us
    dynamic_update_slice x3, local copies, waits for them, and re-layouts, add_block(): lax.dynamic_update_slice(accum, current + block[index], (anchor, anchor,...  14.5 us
    ppermute x6, waiting for transfers between devices, from_behind(): lax.ppermute(value, axis, [(source, source + steps) for source in range(i...  7.43 us
    scatter x1, local copies, waits for them, and re-layouts, place(): return lax.dynamic_update_slice(empty, piece, (anchor, row_at, anchor))  4.84 us
    add x1, other arithmetic, shards(): updated = object_tiles + gradient / (cover + ALPHA)  4.51 us
  transfers between devices with their start and end apart: 8, of which 4 were waited for; matrix products, arithmetic and copies ran while one was open for 9% of the time, Pallas kernels for 0%

profile of v1, /device:TPU:0, one launch (start us, length us, event | category | flops | bytes accessed | tf_op | source)
XLA Modules:
  0.0 165.0 jit_solution(13570193522093173880)
XLA Ops:
  9.3 5.4 %collective-permute-start.2 = (s32[1]{0:T(128)}, s32[1]{0:T(128)}, u32[]{:S(2)}, u32[]{:S(2)}) collective-permute-start(s32[1]{0:T(128)} %bitcast.10), channel_id=1, source_target_pairs={{0,4},{2,6},{4,8},{6,10},{8,12},{10,14},{12,16},{14,18},{16,20},{1... | collective-permute-start | bytes 20 | tf_op jit(solution)/shard_map/ppermute | solution.py:14
  14.7 3.9 %collective-permute-start = (s32[1]{0:T(128)}, s32[1]{0:T(128)}, u32[]{:S(2)}, u32[]{:S(2)}) collective-permute-start(s32[1]{0:T(128)} %bitcast.10), channel_id=1, source_target_pairs={{0,2},{2,4},{4,6},{6,8},{8,10},{10,12},{12,14},{14,16},{16,18},{18... | collective-permute-start | bytes 20 | tf_op jit(solution)/shard_map/ppermute | solution.py:14
  24.3 1.7 %dynamic-slice_bitcast_fusion = (f32[1,2,128,256]{3,2,1,0:T(8,128)S(1)}, f32[1,2,128,256]{3,2,1,0:T(8,128)S(1)}, f32[1,2,128,256]{3,2,1,0:T(8,128)S(1)}) fusion(f32[2,128,2048]{2,1,0:T(8,128)} %param.8, s32[]{:T(128)} %bitcast.15, s32[]{:T(128)} %bitcast.13, s32[]{:T(128)} %bitcast.11), kind=kLoop, calls=%fused_computation.81 | loop fusion | bytes 1572876 | tf_op jit(solution)/shard_map/vmap()/gather | solution.py:55
  29.3 6.1 %collective-permute-done.3 = f32[1,2,128,256]{3,2,1,0:T(8,128)S(1)} collective-permute-done((f32[1,2,128,256]{3,2,1,0:T(8,128)S(1)}, f32[1,2,128,256]{3,2,1,0:T(8,128)S(1)}, u32[]{:S(2)}, u32[]{:S(2)}) %collective-permute-start.3) | collective-permute-done | bytes 262176 | tf_op jit(solution)/shard_map/ppermute | solution.py:14
  37.1 1.6 fusion.46
  38.8 1.6 fusion.42
  43.6 1.6 fusion.4
  48.4 2.5 %add_reduce_fusion = (f32[256,256]{1,0:T(8,128)}, f32[2,256,256]{2,1,0:T(8,128)S(1)}) fusion(f32[2,256,256]{2,1,0:T(8,128)S(1)} %convolution_subtract_fusion.2, f32[2,256,256]{2,1,0:T(8,128)S(1)} %fusion.40, f32[2,256,256]{2,1,0:T(8,128)S(1)} %fusion.5), kind=kOutput, calls=%fused_computation.41 | convolution fusion | flops 404291584 | bytes 2359296 | tf_op jit(solution)/shard_map/dot_general | solution.py:25
  52.4 2.7 %and_reduce_fusion = pred[]{:T(512)} fusion(s32[4]{0:T(128)S(1)} %copy-done.3, s32[1]{0:T(128)} %bitcast.7, s32[1]{0:T(128)} %bitcast.6, s32[1]{0:T(128)} %bitcast.5, s32[1]{0:T(128)} %constant.96.clone.1), kind=kLoop, calls=%fused_computation.118 | loop fusion | flops 27 | bytes 33 | tf_op jit(solution)/shard_map/reduce.1
  55.1 18.5 %all-reduce.6.cloned.1.call-done = f32[1,256,256]{2,1,0:T(8,128)} async-done(((f32[1,256,256]{2,1,0:T(8,128)}), f32[1,256,256]{2,1,0:T(8,128)}) %all-reduce.6.cloned.1.call-update) | async-done | bytes 262160 | tf_op jit(solution)/shard_map/psum | solution.py:75
  74.6 1.7 %fusion.21 = f32[256,2,256]{2,0,1:T(8,128)S(1)} fusion(f32[2,256,256]{2,1,0:T(8,128)S(1)} %convolution_subtract_fusion.2, f32[256,256]{1,0:T(8,128)S(1)} %multiply_bitcast_fusion.3), kind=kOutput, calls=%fused_computation.46 | convolution fusion | flops 403767296 | bytes 1310720 | tf_op jit(solution)/shard_map/dot_general | solution.py:25
  76.2 1.6 fusion.17
  77.9 1.7 %fusion.2 = f32[2,256,256]{2,1,0:T(8,128)S(1)} fusion(f32[256,2,256]{2,0,1:T(8,128)S(1)} %fusion.17, f32[2,256,256]{2,1,0:T(8,128)S(1)} %convolution_subtract_fusion.2, f32[256,256]{1,0:T(8,128)S(1)} %multiply_bitcast_fusion.3), kind=kOutput, calls=%fused_computation.6 | convolution fusion | flops 404029440 | bytes 1835008 | tf_op jit(solution)/shard_map/dot_general | solution.py:25
  79.6 1.7 %fusion.3 = f32[2,256,256]{2,1,0:T(8,128)S(1)} fusion(f32[256,2,256]{2,0,1:T(8,128)S(1)} %fusion.21, f32[2,256,256]{2,1,0:T(8,128)S(1)} %get-tuple-element.133, f32[256,256]{1,0:T(8,128)S(1)} %multiply_bitcast_fusion.3), kind=kOutput, calls=%fused_computation.8 | convolution fusion | flops 404029440 | bytes 1835008 | tf_op jit(solution)/shard_map/dot_general | solution.py:25
  85.9 1.9 %fusion.12 = (f32[256,256]{1,0:T(8,128)S(1)}, f32[256,256]{1,0:T(8,128)S(1)}, f32[256,256]{1,0:T(8,128)S(1)}) fusion(f32[2,256,256]{2,1,0:T(8,128)S(1)} %fusion.1, f32[2,2,256,256]{3,2,1,0:T(8,128)S(1)} %copy-done.1, f32[2,256,256]{2,1,0:T(8,128)S(1)} %get-tuple-element.121, f32[2,256,256]{2,1,0:T(8,128)S(1)} %fusion.34, f32[2,256,256]{2,1,0:T(8,128)S(1)} %fusion.3), kind=kOutput, calls=%fused_computation.31 | convolution fusion | flops 405405696 | bytes 3932160 | tf_op jit(solution)/shard_map/dot_general | solution.py:25
  87.9 2.2 %all-gather = f32[512,256]{1,0:T(8,128)S(1)} all-gather(f32[256,256]{1,0:T(8,128)S(1)} %get-tuple-element.116), channel_id=2, replica_groups=mesh['tile'=16,'mode'=2] {'mode'}, dimensions={0}, use_global_device_ids=true | all-gather | bytes 786432 | tf_op jit(solution)/shard_map/all_gather | solution.py:47
  90.9 4.8 %scatter.4 = f32[1,3,384,256]{3,2,1,0:T(8,128)S(1)} dynamic-update-slice(f32[1,3,384,256]{3,2,1,0:T(8,128)S(1)} %broadcast_in_dim.32, f32[1,3,256,256]{3,2,1,0:T(8,128)S(1)} %maximum_select_fusion, s32[]{:T(128)} %constant.95.clone.1, s32[]{:T(128)} %constant.95.clone.1, s32[]{:T(128)} %bitcast.50, s32[]{:T(128)} %constant.95.clone.1) | dynamic-update-slice | bytes 1572868 | tf_op jit(solution)/shard_map/vmap(vmap())/scatter | solution.py:89
  96.8 3.8 %collective-permute-start.4 = (f32[1,3,128,256]{3,2,1,0:T(8,128)}, f32[1,3,128,256]{3,2,1,0:T(8,128)}, u32[]{:S(2)}, u32[]{:S(2)}) collective-permute-start(f32[1,3,128,256]{3,2,1,0:T(8,128)} %get-tuple-element.123), channel_id=1, source_target_pairs={{0,2},{2,4},{4,6},{6,8},{8,10},{10,12},{12,14},{14,16},{16,18},{18... | collective-permute-start | bytes 1179656 | tf_op jit(solution)/shard_map/ppermute | solution.py:14
  100.6 3.8 %collective-permute-start.5 = (f32[1,3,128,256]{3,2,1,0:T(8,128)}, f32[1,3,128,256]{3,2,1,0:T(8,128)}, u32[]{:S(2)}, u32[]{:S(2)}) collective-permute-start(f32[1,3,128,256]{3,2,1,0:T(8,128)} %get-tuple-element.122), channel_id=1, source_target_pairs={{0,4},{2,6},{4,8},{6,10},{8,12},{10,14},{12,16},{14,18},{16,20},{1... | collective-permute-start | bytes 1179656 | tf_op jit(solution)/shard_map/ppermute | solution.py:14
  110.4 4.8 %dynamic_update_slice.12 = f32[3,128,2048]{2,1,0:T(8,128)S(1)} dynamic-update-slice(f32[3,128,2048]{2,1,0:T(8,128)S(1)} %broadcast_in_dim.31, f32[3,128,256]{2,1,0:T(8,128)S(1)} %get-tuple-element.124, s32[]{:T(128)} %constant.95.clone.1, s32[]{:T(128)} %constant.95.clone.1, s32[]{:T(128)S(6)} %select_n.101) | dynamic-update-slice | bytes 786436 | tf_op jit(solution)/shard_map/while/body/eval_jaxpr/dynamic_update_slice | solution.py:105
  116.4 4.8 %dynamic_update_slice.13 = f32[3,128,2048]{2,1,0:T(8,128)S(1)} dynamic-update-slice(f32[3,128,2048]{2,1,0:T(8,128)S(1)} %dynamic_update_slice.12, f32[3,128,256]{2,1,0:T(8,128)S(1)} %bitcast_add_fusion.1, s32[]{:T(128)} %constant.95.clone.1, s32[]{:T(128)} %constant.95.clone.1, s32[]{:T(128)S(6)} %select_n.102) | dynamic-update-slice | bytes 786436 | tf_op jit(solution)/shard_map/while/body/eval_jaxpr/dynamic_update_slice | solution.py:105
  122.4 4.8 %dynamic_update_slice.14 = f32[3,128,2048]{2,1,0:T(8,128)S(1)} dynamic-update-slice(f32[3,128,2048]{2,1,0:T(8,128)S(1)} %dynamic_update_slice.13, f32[3,128,256]{2,1,0:T(8,128)S(1)} %bitcast_add_fusion, s32[]{:T(128)} %constant.95.clone.1, s32[]{:T(128)} %constant.95.clone.1, s32[]{:T(128)S(6)} %select_n.103) | dynamic-update-slice | bytes 786436 | tf_op jit(solution)/shard_map/while/body/eval_jaxpr/dynamic_update_slice | solution.py:105
  129.8 22.5 %all-reduce.8.cloned.1.call-done = f32[2,128,2048]{2,1,0:T(8,128)} async-done(((f32[2,128,2048]{2,1,0:T(8,128)}), f32[2,128,2048]{2,1,0:T(8,128)}) %all-reduce.8.cloned.1.call-update) | async-done | bytes 2097168 | tf_op jit(solution)/shard_map/psum | solution.py:112
  152.3 4.5 %divide_add_fusion = f32[2,128,2048]{2,1,0:T(8,128)} fusion(f32[2,128,2048]{2,1,0:T(8,128)} %param.8, f32[2,128,2048]{2,1,0:T(8,128)} %all-reduce.8.cloned.1.call-done, f32[128,2048]{1,0:T(8,128)} %fusion.6), kind=kLoop, calls=%fused_computation | loop fusion | flops 1048576 | bytes 7340032 | tf_op jit(solution)/shard_map/add | solution.py:113
  (48 shorter events, 26.9 us)
Async XLA Ops:
  7.2 29.8 %copy-start.1 = (f32[2,2,256,256]{3,2,1,0:T(8,128)S(1)}, f32[2,2,256,256]{3,2,1,0:T(8,128)}, u32[]{:S(2)}) copy-start(f32[2,2,256,256]{3,2,1,0:T(8,128)} %param.9) | copy-start | bytes 3145732
  7.2 66.4 %all-reduce.6.cloned.1.call-start = ((), (), s32[]{:S(2)}) async-start(), calls=%async_computation | async-start | bytes 524288 | tf_op jit(solution)/shard_map/psum | solution.py:75
  9.3 11.2 %collective-permute-start.2 = (s32[1]{0:T(128)}, s32[1]{0:T(128)}, u32[]{:S(2)}, u32[]{:S(2)}) collective-permute-start(s32[1]{0:T(128)} %bitcast.10), channel_id=1, source_target_pairs={{0,4},{2,6},{4,8},{6,10},{8,12},{10,14},{12,16},{14,18},{16,20},{1... | collective-permute-start | bytes 20 | tf_op jit(solution)/shard_map/ppermute | solution.py:14
  14.7 7.1 %collective-permute-start = (s32[1]{0:T(128)}, s32[1]{0:T(128)}, u32[]{:S(2)}, u32[]{:S(2)}) collective-permute-start(s32[1]{0:T(128)} %bitcast.10), channel_id=1, source_target_pairs={{0,2},{2,4},{4,6},{6,8},{8,10},{10,12},{12,14},{14,16},{16,18},{18... | collective-permute-start | bytes 20 | tf_op jit(solution)/shard_map/ppermute | solution.py:14
  26.0 9.4 %collective-permute-start.3 = (f32[1,2,128,256]{3,2,1,0:T(8,128)S(1)}, f32[1,2,128,256]{3,2,1,0:T(8,128)S(1)}, u32[]{:S(2)}, u32[]{:S(2)}) collective-permute-start(f32[1,2,128,256]{3,2,1,0:T(8,128)S(1)} %get-tuple-element.117), channel_id=1, source_target_pairs={{4,0},{6,2},{8,4},{10,6},{12,8},{14,10},{16,12},{18,14},{20,16},{2... | collective-permute-start | bytes 786440 | tf_op jit(solution)/shard_map/ppermute | solution.py:14
  27.3 9.4 %collective-permute-start.1 = (f32[1,2,128,256]{3,2,1,0:T(8,128)S(1)}, f32[1,2,128,256]{3,2,1,0:T(8,128)S(1)}, u32[]{:S(2)}, u32[]{:S(2)}) collective-permute-start(f32[1,2,128,256]{3,2,1,0:T(8,128)S(1)} %get-tuple-element.118), channel_id=1, source_target_pairs={{2,0},{4,2},{6,4},{8,6},{10,8},{12,10},{14,12},{16,14},{18,16},{20... | collective-permute-start | bytes 786440 | tf_op jit(solution)/shard_map/ppermute | solution.py:14
  46.8 4.2 %copy-start.4 = (s32[1,3]{1,0:T(1,128)S(1)}, s32[1,3]{1,0:T(1,128)}, u32[]{:S(2)}) copy-start(s32[1,3]{1,0:T(1,128)} %constant.105.clone.1) | copy-start | bytes 40
  46.8 5.6 %copy-start.3 = (s32[4]{0:T(128)S(1)}, s32[4]{0:T(128)}, u32[]{:S(2)}) copy-start(s32[4]{0:T(128)} %constant.106.clone.1) | copy-start | bytes 52
  46.9 26.7 %copy-start.2 = (f32[1,256,256]{2,1,0:T(8,128)S(1)}, f32[1,256,256]{2,1,0:T(8,128)}, u32[]{:S(2)}) copy-start(f32[1,256,256]{2,1,0:T(8,128)} %param.10) | copy-start | bytes 786436
  50.9 101.3 %all-reduce.8.cloned.1.call-start = ((), (), s32[]{:S(2)}) async-start(), calls=%async_computation.1 | async-start | bytes 4194304 | tf_op jit(solution)/shard_map/psum | solution.py:112
  96.8 18.4 %collective-permute-start.4 = (f32[1,3,128,256]{3,2,1,0:T(8,128)}, f32[1,3,128,256]{3,2,1,0:T(8,128)}, u32[]{:S(2)}, u32[]{:S(2)}) collective-permute-start(f32[1,3,128,256]{3,2,1,0:T(8,128)} %get-tuple-element.123), channel_id=1, source_target_pairs={{0,2},{2,4},{4,6},{6,8},{8,10},{10,12},{12,14},{14,16},{16,18},{18... | collective-permute-start | bytes 1179656 | tf_op jit(solution)/shard_map/ppermute | solution.py:14
  100.6 20.6 %collective-permute-start.5 = (f32[1,3,128,256]{3,2,1,0:T(8,128)}, f32[1,3,128,256]{3,2,1,0:T(8,128)}, u32[]{:S(2)}, u32[]{:S(2)}) collective-permute-start(f32[1,3,128,256]{3,2,1,0:T(8,128)} %get-tuple-element.122), channel_id=1, source_target_pairs={{0,4},{2,6},{4,8},{6,10},{8,12},{10,14},{12,16},{14,18},{16,20},{1... | collective-permute-start | bytes 1179656 | tf_op jit(solution)/shard_map/ppermute | solution.py:14
  152.3 4.5 %copy-start = (f32[2,128,2048]{2,1,0:T(8,128)S(1)}, f32[2,128,2048]{2,1,0:T(8,128)}, u32[]{:S(2)}) copy-start(f32[2,128,2048]{2,1,0:T(8,128)} %all-reduce.8.cloned.1.call-done) | copy-start | bytes 6291460
Sparse Core Ops, SparseCore 0:
  51.1 22.4 all-reduce.5
  128.9 23.3 all-reduce.7
